TPU v7x, 512 devices: a whole 4x8x8 slice. The times are simulated.
512 devices in a mesh: seq: 64 (over z_hi, x, y), width: 8 (over z_lo, core).
Axes of the slice: x: 4, y: 8, z: 8 (z_hi: 2, z_lo: 4; z = z_hi * 4 + z_lo), core: 2. Of those that a mesh axis runs over, the one named last changes fastest.
Arguments:
- projected: bfloat16 [32768, 3, 4096], P('seq', None, 'width'), may hold values from -6 to 6
- short_filter: float32 [3, 3, 4096], P(None, None, 'width'), may hold values from -3.5 to 3.5
- long_filter: bfloat16 [256, 128], P('width'), may hold values from -0.5 to 0.5
- out_weight: bfloat16 [4096, 4096], P('seq', 'width'), may hold values from -0.09375 to 0.09375
Outputs:
- mixed: bfloat16 [32768, 4096], P('seq', 'width')
All inputs are finite; a program needn't handle non-finite values.
Results may differ from a plain program's by a relative error of at most 0.0057.
Values may be sent and summed in bfloat16 or wider, within the bound.
No kernel may reach another device: no remote copies, remote signals or barrier semaphores. Data moves between devices by JAX's collectives and lax.ppermute only.
A program may use at most 64 MiB of HBM per device.

v0:
```python
import jax
import jax.numpy as jnp
from jax import lax
from jax.sharding import PartitionSpec as P


def from_behind(array, axis, by):
    devices = lax.axis_size(axis)
    pairs = [(i, i + by) for i in range(devices) if 0 <= i + by < devices]
    return lax.ppermute(array, axis, pairs)


def featurize_joined(joined, short_filter):
    values = joined.astype(jnp.float32)
    return (
        short_filter[0] * values[2:]
        + short_filter[1] * values[1:-1]
        + short_filter[2] * values[:-2]
    )


def toeplitz_of(long_filter):
    span = long_filter.shape[1]
    row_ids = jnp.arange(span, dtype=jnp.int32)[:, None]
    col_ids = jnp.arange(2 * span - 1, dtype=jnp.int32)[None, :]
    tap_index = row_ids - col_ids + (span - 1)
    inside = (tap_index >= 0) & (tap_index < span)
    picked = jnp.take(long_filter, jnp.clip(tap_index, 0, span - 1), axis=1)
    return jnp.where(inside[None], picked, jnp.zeros_like(picked))


def long_conv(extended, toeplitz, out_rows):
    span = toeplitz.shape[1]
    groups = toeplitz.shape[0]
    channels = extended.shape[1]

    def one_block(block_index):
        window_rows = lax.dynamic_slice_in_dim(extended, block_index * span, 2 * span - 1, 0)
        window_rows = window_rows.reshape(2 * span - 1, groups, channels // groups)
        result = jnp.einsum(
            "gij,jgc->igc", toeplitz, window_rows, preferred_element_type=jnp.float32
        )
        return result.reshape(span, channels)

    blocks = lax.map(one_block, jnp.arange(out_rows // span, dtype=jnp.int32))
    return blocks.reshape(out_rows, channels)


def on_device(projected, short_filter, long_filter, out_weight):
    tok_rows = projected.shape[0]
    span = long_filter.shape[1]
    tail_rows = projected[tok_rows - span - 1 :]
    previous = from_behind(tail_rows, "seq", 1)
    joined = jnp.concatenate([previous, projected], axis=0)
    featured = featurize_joined(joined, short_filter)
    extended = (featured[:, 1] * featured[:, 2]).astype(jnp.bfloat16)
    query = featured[span - 1 :, 0]
    filtered = long_conv(extended, toeplitz_of(long_filter), tok_rows)
    gated = (query * filtered).astype(jnp.bfloat16)
    gathered = lax.all_gather(gated, "width", axis=1, tiled=True)
    mixed = jnp.dot(
        gathered,
        lax.all_gather(out_weight, "seq", axis=0, tiled=True),
        preferred_element_type=jnp.float32,
    )
    return mixed.astype(jnp.bfloat16)


def solution(mesh):
    in_specs = (
        P("seq", None, "width"),
        P(None, None, "width"),
        P("width", None),
        P("seq", "width"),
    )
    out_specs = P("seq", "width")
    return jax.shard_map(
        on_device, mesh=mesh, in_specs=in_specs, out_specs=out_specs, check_vma=False
    )
```

profile of v0, /device:TPU:2, one launch (start us, length us, event | category | flops | bytes accessed | tf_op | source)
XLA Modules:
  0.0 351.0 jit_solution(13737784177788745816)
XLA Ops:
  6.5 0.0 all-gather.3.cloned.1.call-start
  6.5 1.1 slice.31
  7.6 3.5 collective-permute-start
  11.2 0.7 slice_bitcast_fusion.3
  11.9 0.3 reshape.76
  12.3 0.8 copy.9
  13.1 65.9 %gather_fusion = bf16[32640,32]{1,0:T(8,128)(2,1)} fusion(bf16[32,128]{0,1:T(8,128)(2,1)S(1)} %copy.9, s32[32768]{0:T(1024)S(1)} %pad_clamp_fusion), kind=kCustom, calls=%fused_computation | custom fusion | bytes 4308480 | tf_op jit(solution)/shard_map/jit(_take)/gather | solution.py:28
  79.0 6.9 %copy.10 = bf16[32640,32]{0,1:T(8,128)(2,1)S(1)} copy(bf16[32640,32]{1,0:T(8,128)(2,1)} %gather_fusion) | data formatting | bytes 4177920 | tf_op jit(solution)/shard_map/jit(_take)/gather | solution.py:28
  85.8 7.8 %reshape.79 = bf16[128,255,32]{1,0,2:T(8,128)(2,1)} reshape(bf16[32640,32]{0,1:T(8,128)(2,1)S(1)} %copy.10) | data formatting | bytes 4177920 | tf_op jit(solution)/shard_map/jit(_take)/gather | solution.py:28
  93.6 0.0 copy-start.1
  93.6 0.1 fusion.10
  93.7 1.9 select_bitcast_fusion
  95.7 0.0 collective-permute-done
  95.7 0.0 copy-done.1
  95.7 0.6 maximum_convert_fusion
  96.3 1.2 fusion
  97.4 0.0 copy-start
  97.4 1.9 copy-done
  99.3 0.2 fusion.5
  99.5 12.1 %while.10 = (s32[]{:T(128)}, f32[4,128,512]{2,1,0:T(8,128)}, s32[4]{0:T(128)S(1)}, bf16[639,512]{1,0:T(8,128)(2,1)S(1)}, bf16[32,128,255]{2,1,0:T(8,128)(2,1)S(1...) while((s32[]{:T(128)}, f32[4,128,512]{2,1,0:T(8,128)}, s32[4]{0:T(128)S(1)}, ...), condition=%wide.region_1.2_spmd, body=%wide.region_0.1_spmd.sunk | while | flops 33423364 | bytes 4705947 | solution.py:45
  99.5 0.6 dynamic_slice.11
  100.8 0.1 constant_dynamic-slice_fusion.2
  100.9 0.1 copy.18
  101.0 0.6 fusion.22
  101.6 0.2 copy.19
  101.8 0.8 constant_dynamic-update-slice_fusion.2
  102.6 0.6 dynamic_slice.11
  103.8 0.1 constant_dynamic-slice_fusion.2
  103.9 0.1 copy.18
  104.0 0.6 fusion.22
  104.7 0.2 copy.19
  104.8 0.7 constant_dynamic-update-slice_fusion.2
  105.6 0.6 dynamic_slice.11
  106.9 0.1 constant_dynamic-slice_fusion.2
  106.9 0.1 copy.18
  107.1 0.6 fusion.22
  107.7 0.2 copy.19
  107.9 0.7 constant_dynamic-update-slice_fusion.2
  108.6 0.6 dynamic_slice.11
  109.9 0.1 constant_dynamic-slice_fusion.2
  110.0 0.1 copy.18
  110.1 0.6 fusion.22
  110.7 0.2 copy.19
  110.9 0.7 constant_dynamic-update-slice_fusion.2
  111.6 2.6 fusion.4
  114.2 0.0 all-gather.3.cloned.1.call-update
  114.2 0.0 all-gather.5.cloned.1.call-start
  114.3 0.7 all-gather.5.cloned.1.call-update
  115.0 60.9 %all-gather.3.cloned.1.call-done = bf16[512,4096]{1,0:T(8,128)(2,1)} async-done(((bf16[512,512]{1,0:T(8,128)(2,1)}), bf16[512,4096]{1,0:T(8,128)(2,1)}) %all-gather.3.cloned.1.call-update) | async-done | bytes 4194320 | tf_op jit(solution)/shard_map/all_gather | solution.py:60
  175.9 161.7 %all-gather.5.cloned.1.call-done = bf16[4096,512]{1,0:T(8,128)(2,1)} async-done(((bf16[64,512]{1,0:T(8,128)(2,1)}), bf16[4096,512]{1,0:T(8,128)(2,1)}) %all-gather.5.cloned.1.call-update) | async-done | bytes 4194320 | tf_op jit(solution)/shard_map/all_gather | solution.py:63
  337.6 6.6 %convolution_convert_fusion = bf16[512,512]{1,0:T(8,128)(2,1)} fusion(bf16[512,4096]{1,0:T(8,128)(2,1)} %all-gather.3.cloned.1.call-done, bf16[4096,512]{1,0:T(8,128)(2,1)} %all-gather.5.cloned.1.call-done), kind=kOutput, calls=%fused_computation.12 | convolution fusion | flops 2147745792 | bytes 8912896 | tf_op jit(solution)/shard_map/dot_general | solution.py:61
  (4 shorter events, 0.1 us)
Async XLA Ops:
  6.5 169.4 %all-gather.3.cloned.1.call-start = ((), (), s32[]{:S(2)}) async-start(), calls=%async_computation | async-start | bytes 4718592 | tf_op jit(solution)/shard_map/all_gather | solution.py:60
  7.6 88.0 %collective-permute-start = (bf16[129,3,512]{2,0,1:T(8,128)(2,1)S(1)}, bf16[129,3,512]{2,0,1:T(8,128)(2,1)S(1)}, u32[]{:S(2)}, u32[]{:S(2)}) collective-permute-start(bf16[129,3,512]{2,0,1:T(8,128)(2,1)S(1)} %slice.31), channel_id=1, source_target_pairs={{0,8},{8,16},{16,24},{24,32},{32,40},{40,48},{48,56},{56,64},{64,7... | collective-permute-start | bytes 1188872 | tf_op jit(solution)/shard_map/ppermute | solution.py:10
  93.6 2.0 copy-start.1
  97.4 1.9 copy-start
  114.2 223.3 %all-gather.5.cloned.1.call-start = ((), (), s32[]{:S(2)}) async-start(), calls=%async_computation.1 | async-start | bytes 4259840 | tf_op jit(solution)/shard_map/all_gather | solution.py:63
Sparse Core Ops, SparseCore 0:
  114.4 61.5 all-gather.2
  180.4 157.0 all-gather.4
where the time goes:
time: 351 us
  waiting for transfers between devices  223 us (64%)
  local copies, waits for them, and re-layouts  92.3 us (26%)
  between operations  13.5 us (4%)
  matrix products  9.11 us (3%)
  other arithmetic  6.61 us (2%)
  starting transfers between devices  3.53 us (1%)
    all_gather x1, waiting for transfers between devices, on_device(): lax.all_gather(out_weight, 'seq', axis=0, tiled=True)  162 us
    gather x3, local copies, waits for them, and re-layouts, toeplitz_of(): picked = jnp.take(long_filter, jnp.clip(tap_index, 0, span - 1), axis=1)  80.5 us
    all_gather x1, waiting for transfers between devices, on_device(): gathered = lax.all_gather(gated, 'width', axis=1, tiled=True)  60.9 us
  transfers between devices with their start and end apart: 3, of which 2 were waited for; matrix products, arithmetic and copies ran while one was open for 24% of the time, Pallas kernels for 0%

commit v1 on v0

--- a/solution.py
+++ b/solution.py
@@ -57,7 +57,12 @@
     query = featured[span - 1 :, 0]
     filtered = long_conv(extended, toeplitz_of(long_filter), tok_rows)
     gated = (query * filtered).astype(jnp.bfloat16)
-    gathered = lax.all_gather(gated, "width", axis=1, tiled=True)
+    gathered = jnp.concatenate(
+        lax.all_to_all(
+            jnp.stack(tuple((gated for _ in range(lax.axis_size("width")))), axis=0), "width", 0, 0
+        ),
+        axis=1,
+    )
     mixed = jnp.dot(
         gathered,
         lax.all_gather(out_weight, "seq", axis=0, tiled=True),

time: 351 us -> 254 us (0.72)
  the two profiles are of different devices: /device:TPU:2 before, /device:TPU:1 now
where the time goes in v1:
time: 254 us
  blocking collectives  126 us (50%)
  local copies, waits for them, and re-layouts  93.2 us (37%)
  between operations  13.5 us (5%)
  matrix products  9.16 us (4%)
  other arithmetic  5.83 us (2%)
  starting transfers between devices  4.06 us (2%)
  loops' own time  2.68 us (1%)
    all_to_all x1, blocking collectives, on_device(): lax.all_to_all(jnp.stack(tuple((gated for _ in range(lax.axis_size('width...  126 us
    gather x3, local copies, waits for them, and re-layouts, toeplitz_of(): picked = jnp.take(long_filter, jnp.clip(tap_index, 0, span - 1), axis=1)  80.9 us
    dot_general x1, matrix products, on_device(): jnp.dot(gathered, lax.all_gather(out_weight, 'seq', axis=0, tiled=True),...  6.61 us
  transfers between devices with their start and end apart: 2, of which 0 were waited for; matrix products, arithmetic and copies ran while one was open for 39% of the time, Pallas kernels for 0%

profile of v1, /device:TPU:1, one launch (start us, length us, event | category | flops | bytes accessed | tf_op | source)
XLA Modules:
  0.0 254.0 jit_solution(12429368098740300533)
XLA Ops:
  6.5 0.0 all-gather.2.cloned.1.call-start
  6.5 1.1 slice.31
  7.6 4.1 %collective-permute-start = (bf16[129,3,512]{2,0,1:T(8,128)(2,1)S(1)}, bf16[129,3,512]{2,0,1:T(8,128)(2,1)S(1)}, u32[]{:S(2)}, u32[]{:S(2)}) collective-permute-start(bf16[129,3,512]{2,0,1:T(8,128)(2,1)S(1)} %slice.31), channel_id=1, source_target_pairs={{0,8},{8,16},{16,24},{24,32},{32,40},{40,48},{48,56},{56,64},{64,7... | collective-permute-start | bytes 1188872 | tf_op jit(solution)/shard_map/ppermute | solution.py:10
  11.7 0.0 all-gather.2.cloned.1.call-update
  11.8 0.7 slice_bitcast_fusion.3
  12.5 0.3 reshape.89
  12.9 0.8 copy.10
  13.7 66.3 %gather_fusion = bf16[32640,32]{1,0:T(8,128)(2,1)} fusion(bf16[32,128]{0,1:T(8,128)(2,1)S(1)} %copy.10, s32[32768]{0:T(1024)S(1)} %pad_clamp_fusion), kind=kCustom, calls=%fused_computation | custom fusion | bytes 4308480 | tf_op jit(solution)/shard_map/jit(_take)/gather | solution.py:28
  80.0 6.9 %copy.11 = bf16[32640,32]{0,1:T(8,128)(2,1)S(1)} copy(bf16[32640,32]{1,0:T(8,128)(2,1)} %gather_fusion) | data formatting | bytes 4177920 | tf_op jit(solution)/shard_map/jit(_take)/gather | solution.py:28
  86.8 7.8 %reshape.92 = bf16[128,255,32]{1,0,2:T(8,128)(2,1)} reshape(bf16[32640,32]{0,1:T(8,128)(2,1)S(1)} %copy.11) | data formatting | bytes 4177920 | tf_op jit(solution)/shard_map/jit(_take)/gather | solution.py:28
  94.7 0.0 copy-start.1
  94.7 0.1 fusion.10
  94.8 1.9 select_bitcast_fusion
  96.7 0.0 collective-permute-done
  96.7 0.0 copy-done.1
  96.7 0.6 maximum_convert_fusion
  97.3 1.2 fusion
  98.5 0.0 copy-start
  98.5 1.9 copy-done
  100.3 0.2 fusion.5
  100.5 12.0 %while.10 = (s32[]{:T(128)}, f32[4,128,512]{2,1,0:T(8,128)}, s32[4]{0:T(128)S(1)}, bf16[639,512]{1,0:T(8,128)(2,1)S(1)}, bf16[32,128,255]{2,1,0:T(8,128)(2,1)S(1...) while((s32[]{:T(128)}, f32[4,128,512]{2,1,0:T(8,128)}, s32[4]{0:T(128)S(1)}, ...), condition=%wide.region_1.2_spmd, body=%wide.region_0.1_spmd.sunk | while | flops 33423364 | bytes 4705947 | solution.py:45
  100.5 0.6 dynamic_slice.11
  101.8 0.1 constant_dynamic-slice_fusion.2
  101.9 0.1 copy.20
  102.0 0.7 fusion.22
  102.7 0.1 copy.21
  102.8 0.7 constant_dynamic-update-slice_fusion.2
  103.5 0.6 dynamic_slice.11
  104.8 0.1 constant_dynamic-slice_fusion.2
  104.9 0.1 copy.20
  105.0 0.6 fusion.22
  105.7 0.2 copy.21
  105.8 0.8 constant_dynamic-update-slice_fusion.2
  106.6 0.6 dynamic_slice.11
  107.8 0.1 constant_dynamic-slice_fusion.2
  107.9 0.1 copy.20
  108.0 0.6 fusion.22
  108.7 0.2 copy.21
  108.8 0.7 constant_dynamic-update-slice_fusion.2
  109.6 0.6 dynamic_slice.11
  110.8 0.1 constant_dynamic-slice_fusion.2
  110.9 0.1 copy.20
  111.1 0.6 fusion.22
  111.7 0.2 copy.21
  111.8 0.7 constant_dynamic-update-slice_fusion.2
  112.6 1.8 fusion.4
  114.4 0.2 copy.14
  114.6 0.4 stack.2
  115.0 125.6 %all_to_all.5 = bf16[8,512,512]{1,2,0:T(8,128)(2,1)} all-to-all(bf16[8,512,512]{1,2,0:T(8,128)(2,1)S(1)} %stack.2), channel_id=1, replica_groups=mesh['seq'=64,'width'=8] {'width'}, dimensions={0} | all-to-all | bytes 8388608 | tf_op jit(solution)/shard_map/all_to_all | solution.py:61
  240.5 0.0 all-gather.2.cloned.1.call-done
  240.6 6.6 %convolution_convert_fusion = bf16[512,512]{1,0:T(8,128)(2,1)} fusion(bf16[512,4096]{0,1:T(8,128)(2,1)} %bitcast.46, bf16[4096,512]{1,0:T(8,128)(2,1)} %all-gather.2.cloned.1.call-done), kind=kOutput, calls=%fused_computation.12 | convolution fusion | flops 2147745792 | bytes 8912896 | tf_op jit(solution)/shard_map/dot_general | solution.py:66
  (4 shorter events, 0.1 us)
Async XLA Ops:
  6.5 234.0 %all-gather.2.cloned.1.call-start = ((), (), s32[]{:S(2)}) async-start(), calls=%async_computation.1 | async-start | bytes 4259840 | tf_op jit(solution)/shard_map/all_gather | solution.py:68
  7.6 89.1 %collective-permute-start = (bf16[129,3,512]{2,0,1:T(8,128)(2,1)S(1)}, bf16[129,3,512]{2,0,1:T(8,128)(2,1)S(1)}, u32[]{:S(2)}, u32[]{:S(2)}) collective-permute-start(bf16[129,3,512]{2,0,1:T(8,128)(2,1)S(1)} %slice.31), channel_id=1, source_target_pairs={{0,8},{8,16},{16,24},{24,32},{32,40},{40,48},{48,56},{56,64},{64,7... | collective-permute-start | bytes 1188872 | tf_op jit(solution)/shard_map/ppermute | solution.py:10
  94.7 2.1 copy-start.1
  98.5 1.9 copy-start
Sparse Core Ops, SparseCore 0:
  11.9 160.3 all-gather.1
